TPU v7x, 128 devices: a whole 4x4x4 slice. The times are simulated.
128 devices in a mesh: row: 8 (over x, y_lo), col: 16 (over z, y_hi, core).
Axes of the slice: x: 4, y: 4 (y_hi: 2, y_lo: 2; y = y_hi * 2 + y_lo), z: 4, core: 2. Of those that a mesh axis runs over, the one named last changes fastest.
Arguments:
- left_blocks: bfloat16 [8192, 8192], P('row', 'col'), may hold values from -6 to 6
- right_blocks: bfloat16 [8192, 8192], P('row', 'col'), may hold values from -0.09375 to 0.09375
- a_pattern: int32 [64, 64], P('row', 'col'), may hold values from 0 to 1, as said below
- b_pattern: int32 [64, 64], P('row', 'col'), may hold values 0 or 1
- keep_mask: int32 [64, 64], P('row', 'col'), may hold values 0 or 1
Outputs:
- product: bfloat16 [8192, 8192], P('row', 'col')
Inputs may be any that keep to these rules, and one draw needn't show every extreme that they name: 1 marks a stored block; on average the share of stored blocks rises from about a quarter in the first block rows to about nine tenths in the last. A program may rely on no bound on the sum of `a_pattern` on one device or in one block row.
All inputs are finite; a program needn't handle non-finite values. No bound on the sum of `b_pattern` or of `keep_mask` on one device may be relied on, other than what follows from the above.
Results may differ from a plain program's by a relative error of at most 0.001.
Values may be sent and summed in bfloat16 or wider, within the bound.
A program may use at most 128 MiB of HBM per device.

v0:
```python
import jax
import jax.numpy as jnp
from jax import lax
from jax.sharding import PartitionSpec as P


def from_behind(block, axis, distance):
    devices = range(lax.axis_size(axis))
    route = [((i - distance) % len(devices), i) for i in devices]
    return lax.ppermute(block, axis, route)


def expand_blocks(pattern_int, block_size):
    return jnp.repeat(jnp.repeat(pattern_int, block_size, axis=0), block_size, axis=1)


def advance_left(shard_data):
    return from_behind(shard_data, "col", -1)


def on_device(left_blocks, right_blocks, a_pattern, b_pattern, keep_mask):
    block_size = left_blocks.shape[0] // a_pattern.shape[0]
    left_part = left_blocks * expand_blocks(a_pattern, block_size).astype(jnp.bfloat16)
    right_part = right_blocks * expand_blocks(b_pattern, block_size).astype(jnp.bfloat16)
    n_row = lax.axis_size("row")
    n_col = lax.axis_size("col")
    panel_ratio = n_col // n_row
    product_sum = jnp.zeros((left_part.shape[0], right_part.shape[1]), jnp.float32)
    row_place = lax.axis_index("row")
    col_place = lax.axis_index("col")
    left_amount = panel_ratio * row_place % n_col
    for power in range((n_col - 1).bit_length()):
        shifted = from_behind(left_part, "col", -(1 << power))
        left_part = jnp.where(left_amount // (1 << power) % 2 == 1, shifted, left_part)
    right_amount = col_place // panel_ratio % n_row
    for power in range((n_row - 1).bit_length()):
        shifted = from_behind(right_part, "row", -(1 << power))
        right_part = jnp.where(right_amount // (1 << power) % 2 == 1, shifted, right_part)
    panel_rows = right_part.shape[0] // panel_ratio
    following = from_behind(right_part, "row", -1)
    joined = jnp.concatenate([right_part, following], axis=0)
    right_part = lax.dynamic_slice_in_dim(
        joined, col_place % panel_ratio * panel_rows, right_part.shape[0], 0
    )

    def run_group(running, left_now, right_now, final_group):
        for within in range(panel_ratio):
            panel_now = right_now[within * panel_rows : (within + 1) * panel_rows]
            running = running + jnp.dot(left_now, panel_now, preferred_element_type=jnp.float32)
            if not final_group or within < panel_ratio - 1:
                left_now = advance_left(left_now)
        return (running, left_now)

    def advance_group(group_index, carried):
        running, left_now, right_now = carried
        running, left_now = run_group(running, left_now, right_now, False)
        right_now = from_behind(right_now, "row", -1)
        return (running, left_now, right_now)

    product_sum, left_part, right_part = lax.fori_loop(
        0, n_row - 1, advance_group, (product_sum, left_part, right_part)
    )
    product_sum, left_part = run_group(product_sum, left_part, right_part, True)
    kept_cells = expand_blocks(keep_mask, block_size).astype(jnp.float32)
    return (product_sum * kept_cells).astype(jnp.bfloat16)


def solution(mesh):
    placed = (P("row", "col"), P("row", "col"), P("row", "col"), P("row", "col"), P("row", "col"))
    return jax.shard_map(
        on_device, mesh=mesh, in_specs=placed, out_specs=P("row", "col"), check_vma=False
    )
```

profile of v0, /device:TPU:1, one launch (start us, length us, event | category | flops | bytes accessed | tf_op | source)
XLA Modules:
  0.0 532.6 jit_solution(261388369040371538)
XLA Ops:
  0.9 2.9 broadcast_in_dim.25
  4.1 4.4 collective-permute-start.7
  8.6 2.9 broadcast_in_dim.23
  12.8 17.6 %collective-permute-done.7 = bf16[1024,512]{1,0:T(8,128)(2,1)} collective-permute-done((bf16[1024,512]{1,0:T(8,128)(2,1)S(1)}, bf16[1024,512]{1,0:T(8,128)(2,1)}, u32[]{:S(2)}, u32[]{:S(2)}) %collective-permute-start.7) | collective-permute-done | bytes 1048608 | tf_op jit(solution)/shard_map/ppermute | solution.py:10
  30.4 1.3 collective-permute-start.8
  31.8 12.8 %collective-permute-done.3 = bf16[1024,512]{1,0:T(8,128)(2,1)} collective-permute-done((bf16[1024,512]{1,0:T(8,128)(2,1)S(1)}, bf16[1024,512]{1,0:T(8,128)(2,1)}, u32[]{:S(2)}, u32[]{:S(2)}) %collective-permute-start.3) | collective-permute-done | bytes 1048608 | tf_op jit(solution)/shard_map/ppermute | solution.py:10
  45.6 2.5 collective-permute-start.4
  48.1 5.6 %collective-permute-done.8 = bf16[1024,512]{1,0:T(8,128)(2,1)} collective-permute-done((bf16[1024,512]{1,0:T(8,128)(2,1)S(1)}, bf16[1024,512]{1,0:T(8,128)(2,1)}, u32[]{:S(2)}, u32[]{:S(2)}) %collective-permute-start.8) | collective-permute-done | bytes 1048608 | tf_op jit(solution)/shard_map/ppermute | solution.py:10
  53.8 1.6 collective-permute-start.9
  55.4 14.9 %collective-permute-done.4 = bf16[1024,512]{1,0:T(8,128)(2,1)} collective-permute-done((bf16[1024,512]{1,0:T(8,128)(2,1)}, bf16[1024,512]{1,0:T(8,128)(2,1)}, u32[]{:S(2)}, u32[]{:S(2)}) %collective-permute-start.4) | collective-permute-done | bytes 1048608 | tf_op jit(solution)/shard_map/ppermute | solution.py:10
  70.3 1.3 broadcast_select_fusion.4
  71.7 3.8 collective-permute-start.5
  75.5 2.2 collective-permute-done.9
  77.8 5.6 %collective-permute-start.10 = (bf16[1024,512]{1,0:T(8,128)(2,1)S(1)}, bf16[1024,512]{1,0:T(8,128)(2,1)}, u32[]{:S(2)}, u32[]{:S(2)}) collective-permute-start(bf16[1024,512]{1,0:T(8,128)(2,1)S(1)} %broadcast_select_fusion.2), channel_id=1, source_target_pairs={{16,0},{32,16},{48,32},{64,48},{80,64},{96,80},{112,96},{0,112},{1... | collective-permute-start | bytes 3145736 | tf_op jit(solution)/shard_map/ppermute | solution.py:10
  83.4 13.5 %collective-permute-done.5 = bf16[1024,512]{1,0:T(8,128)(2,1)} collective-permute-done((bf16[1024,512]{1,0:T(8,128)(2,1)S(1)}, bf16[1024,512]{1,0:T(8,128)(2,1)}, u32[]{:S(2)}, u32[]{:S(2)}) %collective-permute-start.5) | collective-permute-done | bytes 1048608 | tf_op jit(solution)/shard_map/ppermute | solution.py:10
  98.0 2.1 collective-permute-start.6
  100.2 2.2 collective-permute-done.10
  102.4 2.3 fusion.5
  104.7 19.1 %collective-permute-done.6 = bf16[1024,512]{1,0:T(8,128)(2,1)S(1)} collective-permute-done((bf16[1024,512]{1,0:T(8,128)(2,1)}, bf16[1024,512]{1,0:T(8,128)(2,1)S(1)}, u32[]{:S(2)}, u32[]{:S(2)}) %collective-permute-start.6) | collective-permute-done | bytes 1048608 | tf_op jit(solution)/shard_map/ppermute | solution.py:10
  123.8 2.3 broadcast_select_fusion.6
  126.2 387.5 %while.15 = (s32[]{:T(128)}, f32[1024,512]{1,0:T(8,128)}, bf16[1024,512]{1,0:T(8,128)(2,1)}, bf16[1024,512]{1,0:T(8,128)(2,1)S(1)}, s32[]{:T(128)}, /*index=5*/s32[]{:T(128)}) while((s32[]{:T(128)}, f32[1024,512]{1,0:T(8,128)}, bf16[1024,512]{1,0:T(8,128)(2,1)}, bf16[1024,512]{1,0:T(8,128)(2,1)S(1)}, s32[]{:T(128)}, ...), condition=%wide.region_1.2_spmd.clone, body=%wide.region_0.1_spmd.clone.sunk | while | flops 1075314688 | bytes 45089020 | solution.py:60
  127.4 1.5 collective-permute-start
  129.0 1.5 collective-permute-start.2
  130.5 37.3 %collective-permute-done = bf16[1024,512]{1,0:T(8,128)(2,1)} collective-permute-done((bf16[1024,512]{1,0:T(8,128)(2,1)S(1)}, bf16[1024,512]{1,0:T(8,128)(2,1)}, u32[]{:S(2)}, u32[]{:S(2)}) %collective-permute-start) | collective-permute-done | bytes 1048608 | tf_op jit(solution)/shard_map/while/body/eval_jaxpr/ppermute | solution.py:10
  169.4 2.1 fusion.27
  171.5 12.3 %collective-permute-done.1 = bf16[1024,512]{1,0:T(8,128)(2,1)} collective-permute-done((bf16[1024,512]{1,0:T(8,128)(2,1)}, bf16[1024,512]{1,0:T(8,128)(2,1)}, u32[]{:S(2)}, u32[]{:S(2)}) %collective-permute-start.1) | collective-permute-done | bytes 1048608 | tf_op jit(solution)/shard_map/while/body/eval_jaxpr/ppermute | solution.py:10
  185.4 36.7 %collective-permute-done = bf16[1024,512]{1,0:T(8,128)(2,1)} collective-permute-done((bf16[1024,512]{1,0:T(8,128)(2,1)S(1)}, bf16[1024,512]{1,0:T(8,128)(2,1)}, u32[]{:S(2)}, u32[]{:S(2)}) %collective-permute-start) | collective-permute-done | bytes 1048608 | tf_op jit(solution)/shard_map/while/body/eval_jaxpr/ppermute | solution.py:10
  223.8 2.1 fusion.27
  225.9 12.3 %collective-permute-done.1 = bf16[1024,512]{1,0:T(8,128)(2,1)} collective-permute-done((bf16[1024,512]{1,0:T(8,128)(2,1)}, bf16[1024,512]{1,0:T(8,128)(2,1)}, u32[]{:S(2)}, u32[]{:S(2)}) %collective-permute-start.1) | collective-permute-done | bytes 1048608 | tf_op jit(solution)/shard_map/while/body/eval_jaxpr/ppermute | solution.py:10
  239.5 1.4 collective-permute-start
  241.0 36.3 %collective-permute-done = bf16[1024,512]{1,0:T(8,128)(2,1)} collective-permute-done((bf16[1024,512]{1,0:T(8,128)(2,1)S(1)}, bf16[1024,512]{1,0:T(8,128)(2,1)}, u32[]{:S(2)}, u32[]{:S(2)}) %collective-permute-start) | collective-permute-done | bytes 1048608 | tf_op jit(solution)/shard_map/while/body/eval_jaxpr/ppermute | solution.py:10
  278.9 2.1 fusion.27
  281.0 12.3 %collective-permute-done.1 = bf16[1024,512]{1,0:T(8,128)(2,1)} collective-permute-done((bf16[1024,512]{1,0:T(8,128)(2,1)}, bf16[1024,512]{1,0:T(8,128)(2,1)}, u32[]{:S(2)}, u32[]{:S(2)}) %collective-permute-start.1) | collective-permute-done | bytes 1048608 | tf_op jit(solution)/shard_map/while/body/eval_jaxpr/ppermute | solution.py:10
  295.2 37.6 %collective-permute-done = bf16[1024,512]{1,0:T(8,128)(2,1)} collective-permute-done((bf16[1024,512]{1,0:T(8,128)(2,1)S(1)}, bf16[1024,512]{1,0:T(8,128)(2,1)}, u32[]{:S(2)}, u32[]{:S(2)}) %collective-permute-start) | collective-permute-done | bytes 1048608 | tf_op jit(solution)/shard_map/while/body/eval_jaxpr/ppermute | solution.py:10
  334.5 2.1 fusion.27
  336.6 12.3 %collective-permute-done.1 = bf16[1024,512]{1,0:T(8,128)(2,1)} collective-permute-done((bf16[1024,512]{1,0:T(8,128)(2,1)}, bf16[1024,512]{1,0:T(8,128)(2,1)}, u32[]{:S(2)}, u32[]{:S(2)}) %collective-permute-start.1) | collective-permute-done | bytes 1048608 | tf_op jit(solution)/shard_map/while/body/eval_jaxpr/ppermute | solution.py:10
  351.1 37.0 %collective-permute-done = bf16[1024,512]{1,0:T(8,128)(2,1)} collective-permute-done((bf16[1024,512]{1,0:T(8,128)(2,1)S(1)}, bf16[1024,512]{1,0:T(8,128)(2,1)}, u32[]{:S(2)}, u32[]{:S(2)}) %collective-permute-start) | collective-permute-done | bytes 1048608 | tf_op jit(solution)/shard_map/while/body/eval_jaxpr/ppermute | solution.py:10
  389.7 2.1 fusion.27
  391.8 12.3 %collective-permute-done.1 = bf16[1024,512]{1,0:T(8,128)(2,1)} collective-permute-done((bf16[1024,512]{1,0:T(8,128)(2,1)}, bf16[1024,512]{1,0:T(8,128)(2,1)}, u32[]{:S(2)}, u32[]{:S(2)}) %collective-permute-start.1) | collective-permute-done | bytes 1048608 | tf_op jit(solution)/shard_map/while/body/eval_jaxpr/ppermute | solution.py:10
  405.5 38.1 %collective-permute-done = bf16[1024,512]{1,0:T(8,128)(2,1)} collective-permute-done((bf16[1024,512]{1,0:T(8,128)(2,1)S(1)}, bf16[1024,512]{1,0:T(8,128)(2,1)}, u32[]{:S(2)}, u32[]{:S(2)}) %collective-permute-start) | collective-permute-done | bytes 1048608 | tf_op jit(solution)/shard_map/while/body/eval_jaxpr/ppermute | solution.py:10
  445.2 2.1 fusion.27
  447.4 12.3 %collective-permute-done.1 = bf16[1024,512]{1,0:T(8,128)(2,1)} collective-permute-done((bf16[1024,512]{1,0:T(8,128)(2,1)}, bf16[1024,512]{1,0:T(8,128)(2,1)}, u32[]{:S(2)}, u32[]{:S(2)}) %collective-permute-start.1) | collective-permute-done | bytes 1048608 | tf_op jit(solution)/shard_map/while/body/eval_jaxpr/ppermute | solution.py:10
  461.1 36.5 %collective-permute-done = bf16[1024,512]{1,0:T(8,128)(2,1)} collective-permute-done((bf16[1024,512]{1,0:T(8,128)(2,1)S(1)}, bf16[1024,512]{1,0:T(8,128)(2,1)}, u32[]{:S(2)}, u32[]{:S(2)}) %collective-permute-start) | collective-permute-done | bytes 1048608 | tf_op jit(solution)/shard_map/while/body/eval_jaxpr/ppermute | solution.py:10
  499.2 2.1 fusion.27
  501.3 12.3 %collective-permute-done.1 = bf16[1024,512]{1,0:T(8,128)(2,1)} collective-permute-done((bf16[1024,512]{1,0:T(8,128)(2,1)}, bf16[1024,512]{1,0:T(8,128)(2,1)}, u32[]{:S(2)}, u32[]{:S(2)}) %collective-permute-start.1) | collective-permute-done | bytes 1048608 | tf_op jit(solution)/shard_map/while/body/eval_jaxpr/ppermute | solution.py:10
  514.6 1.9 fusion.10
  516.5 13.1 %collective-permute-done.11 = bf16[1024,512]{1,0:T(8,128)(2,1)S(1)} collective-permute-done((bf16[1024,512]{1,0:T(8,128)(2,1)}, bf16[1024,512]{1,0:T(8,128)(2,1)S(1)}, u32[]{:S(2)}, u32[]{:S(2)}) %collective-permute-start.11) | collective-permute-done | bytes 1048608 | tf_op jit(solution)/shard_map/ppermute | solution.py:10
  530.9 1.7 fusion.4
  (104 shorter events, 29.4 us)
Async XLA Ops:
  0.0 3.9 copy-start.3
  0.9 7.5 %copy-start.5 = (s32[8,4]{0,1:T(4,128)S(1)}, s32[8,4]{0,1:T(4,128)}, u32[]{:S(2)}) copy-start(s32[8,4]{0,1:T(4,128)} %param.9) | copy-start | bytes 388
  3.9 7.7 %copy-start.4 = (bf16[1024,512]{1,0:T(8,128)(2,1)S(1)}, bf16[1024,512]{1,0:T(8,128)(2,1)}, u32[]{:S(2)}) copy-start(bf16[1024,512]{1,0:T(8,128)(2,1)} %param.7) | copy-start | bytes 3145732
  4.1 26.3 %collective-permute-start.7 = (bf16[1024,512]{1,0:T(8,128)(2,1)S(1)}, bf16[1024,512]{1,0:T(8,128)(2,1)}, u32[]{:S(2)}, u32[]{:S(2)}) collective-permute-start(bf16[1024,512]{1,0:T(8,128)(2,1)S(1)} %bitcast_multiply_fusion.1), channel_id=1, source_target_pairs={{16,0},{32,16},{48,32},{64,48},{80,64},{96,80},{112,96},{0,112},{1... | collective-permute-start | bytes 3145736 | tf_op jit(solution)/shard_map/ppermute | solution.py:10
  11.7 32.8 %collective-permute-start.3 = (bf16[1024,512]{1,0:T(8,128)(2,1)S(1)}, bf16[1024,512]{1,0:T(8,128)(2,1)}, u32[]{:S(2)}, u32[]{:S(2)}) collective-permute-start(bf16[1024,512]{1,0:T(8,128)(2,1)S(1)} %bitcast_multiply_fusion.2), channel_id=1, source_target_pairs={{1,0},{2,1},{3,2},{4,3},{5,4},{6,5},{7,6},{8,7},{9,8},{10,9},{11,1... | collective-permute-start | bytes 3145736 | tf_op jit(solution)/shard_map/ppermute | solution.py:10
  30.4 23.3 %collective-permute-start.8 = (bf16[1024,512]{1,0:T(8,128)(2,1)S(1)}, bf16[1024,512]{1,0:T(8,128)(2,1)}, u32[]{:S(2)}, u32[]{:S(2)}) collective-permute-start(bf16[1024,512]{1,0:T(8,128)(2,1)S(1)} %broadcast_select_fusion), channel_id=1, source_target_pairs={{32,0},{48,16},{64,32},{80,48},{96,64},{112,80},{0,96},{16,112},{3... | collective-permute-start | bytes 3145736 | tf_op jit(solution)/shard_map/ppermute | solution.py:10
  45.6 24.7 %collective-permute-start.4 = (bf16[1024,512]{1,0:T(8,128)(2,1)}, bf16[1024,512]{1,0:T(8,128)(2,1)}, u32[]{:S(2)}, u32[]{:S(2)}) collective-permute-start(bf16[1024,512]{1,0:T(8,128)(2,1)} %broadcast_select_fusion.3), channel_id=1, source_target_pairs={{2,0},{3,1},{4,2},{5,3},{6,4},{7,5},{8,6},{9,7},{10,8},{11,9},{12,... | collective-permute-start | bytes 3145736 | tf_op jit(solution)/shard_map/ppermute | solution.py:10
  53.8 23.9 %collective-permute-start.9 = (bf16[1024,512]{1,0:T(8,128)(2,1)S(1)}, bf16[1024,512]{1,0:T(8,128)(2,1)}, u32[]{:S(2)}, u32[]{:S(2)}) collective-permute-start(bf16[1024,512]{1,0:T(8,128)(2,1)S(1)} %broadcast_select_fusion.1), channel_id=1, source_target_pairs={{64,0},{80,16},{96,32},{112,48},{0,64},{16,80},{32,96},{48,112},{6... | collective-permute-start | bytes 3145736 | tf_op jit(solution)/shard_map/ppermute | solution.py:10
  71.7 25.3 %collective-permute-start.5 = (bf16[1024,512]{1,0:T(8,128)(2,1)S(1)}, bf16[1024,512]{1,0:T(8,128)(2,1)}, u32[]{:S(2)}, u32[]{:S(2)}) collective-permute-start(bf16[1024,512]{1,0:T(8,128)(2,1)S(1)} %broadcast_select_fusion.4), channel_id=1, source_target_pairs={{4,0},{5,1},{6,2},{7,3},{8,4},{9,5},{10,6},{11,7},{12,8},{13,9},{1... | collective-permute-start | bytes 3145736 | tf_op jit(solution)/shard_map/ppermute | solution.py:10
  77.8 24.6 %collective-permute-start.10 = (bf16[1024,512]{1,0:T(8,128)(2,1)S(1)}, bf16[1024,512]{1,0:T(8,128)(2,1)}, u32[]{:S(2)}, u32[]{:S(2)}) collective-permute-start(bf16[1024,512]{1,0:T(8,128)(2,1)S(1)} %broadcast_select_fusion.2), channel_id=1, source_target_pairs={{16,0},{32,16},{48,32},{64,48},{80,64},{96,80},{112,96},{0,112},{1... | collective-permute-start | bytes 3145736 | tf_op jit(solution)/shard_map/ppermute | solution.py:10
  98.0 25.8 %collective-permute-start.6 = (bf16[1024,512]{1,0:T(8,128)(2,1)}, bf16[1024,512]{1,0:T(8,128)(2,1)S(1)}, u32[]{:S(2)}, u32[]{:S(2)}) collective-permute-start(bf16[1024,512]{1,0:T(8,128)(2,1)} %broadcast_select_fusion.5), channel_id=1, source_target_pairs={{8,0},{9,1},{10,2},{11,3},{12,4},{13,5},{14,6},{15,7},{0,8},{1,9},... | collective-permute-start | bytes 3145736 | tf_op jit(solution)/shard_map/ppermute | solution.py:10
  126.2 388.3 %copy-start.6 = (s32[8,4]{0,1:T(4,128)S(1)}, s32[8,4]{0,1:T(4,128)}, u32[]{:S(2)}) copy-start(s32[8,4]{0,1:T(4,128)} %param.11) | copy-start | bytes 388
  127.4 40.4 %collective-permute-start = (bf16[1024,512]{1,0:T(8,128)(2,1)S(1)}, bf16[1024,512]{1,0:T(8,128)(2,1)}, u32[]{:S(2)}, u32[]{:S(2)}) collective-permute-start(bf16[1024,512]{1,0:T(8,128)(2,1)S(1)} %copy.21), channel_id=1, source_target_pairs={{1,0},{2,1},{3,2},{4,3},{5,4},{6,5},{7,6},{8,7},{9,8},{10,9},{11,1... | collective-permute-start | bytes 3145736 | tf_op jit(solution)/shard_map/while/body/eval_jaxpr/ppermute | solution.py:10
  129.0 42.5 %collective-permute-start.2 = (bf16[1024,512]{1,0:T(8,128)(2,1)S(1)}, bf16[1024,512]{1,0:T(8,128)(2,1)S(1)}, u32[]{:S(2)}, u32[]{:S(2)}) collective-permute-start(bf16[1024,512]{1,0:T(8,128)(2,1)S(1)} %copy.22), channel_id=1, source_target_pairs={{16,0},{32,16},{48,32},{64,48},{80,64},{96,80},{112,96},{0,112},{1... | collective-permute-start | bytes 3145736 | tf_op jit(solution)/shard_map/while/body/eval_jaxpr/ppermute | solution.py:10
  167.8 16.0 %collective-permute-start.1 = (bf16[1024,512]{1,0:T(8,128)(2,1)}, bf16[1024,512]{1,0:T(8,128)(2,1)}, u32[]{:S(2)}, u32[]{:S(2)}) collective-permute-start(bf16[1024,512]{1,0:T(8,128)(2,1)} %collective-permute-done), channel_id=1, source_target_pairs={{1,0},{2,1},{3,2},{4,3},{5,4},{6,5},{7,6},{8,7},{9,8},{10,9},{11,1... | collective-permute-start | bytes 3145736 | tf_op jit(solution)/shard_map/while/body/eval_jaxpr/ppermute | solution.py:10
  167.8 1.6 copy-start
  171.5 12.4 %copy-start.1 = (f32[1024,512]{1,0:T(8,128)}, f32[1024,512]{1,0:T(8,128)S(1)}, u32[]{:S(2)}) copy-start(f32[1024,512]{1,0:T(8,128)S(1)} %fusion.27) | copy-start | bytes 6291460 | tf_op jit(solution)/shard_map/while
  185.1 37.1 %collective-permute-start = (bf16[1024,512]{1,0:T(8,128)(2,1)S(1)}, bf16[1024,512]{1,0:T(8,128)(2,1)}, u32[]{:S(2)}, u32[]{:S(2)}) collective-permute-start(bf16[1024,512]{1,0:T(8,128)(2,1)S(1)} %copy.21), channel_id=1, source_target_pairs={{1,0},{2,1},{3,2},{4,3},{5,4},{6,5},{7,6},{8,7},{9,8},{10,9},{11,1... | collective-permute-start | bytes 3145736 | tf_op jit(solution)/shard_map/while/body/eval_jaxpr/ppermute | solution.py:10
  185.4 40.5 %collective-permute-start.2 = (bf16[1024,512]{1,0:T(8,128)(2,1)S(1)}, bf16[1024,512]{1,0:T(8,128)(2,1)S(1)}, u32[]{:S(2)}, u32[]{:S(2)}) collective-permute-start(bf16[1024,512]{1,0:T(8,128)(2,1)S(1)} %copy.22), channel_id=1, source_target_pairs={{16,0},{32,16},{48,32},{64,48},{80,64},{96,80},{112,96},{0,112},{1... | collective-permute-start | bytes 3145736 | tf_op jit(solution)/shard_map/while/body/eval_jaxpr/ppermute | solution.py:10
  222.2 16.0 %collective-permute-start.1 = (bf16[1024,512]{1,0:T(8,128)(2,1)}, bf16[1024,512]{1,0:T(8,128)(2,1)}, u32[]{:S(2)}, u32[]{:S(2)}) collective-permute-start(bf16[1024,512]{1,0:T(8,128)(2,1)} %collective-permute-done), channel_id=1, source_target_pairs={{1,0},{2,1},{3,2},{4,3},{5,4},{6,5},{7,6},{8,7},{9,8},{10,9},{11,1... | collective-permute-start | bytes 3145736 | tf_op jit(solution)/shard_map/while/body/eval_jaxpr/ppermute | solution.py:10
  222.2 1.6 copy-start
  225.9 12.4 %copy-start.1 = (f32[1024,512]{1,0:T(8,128)}, f32[1024,512]{1,0:T(8,128)S(1)}, u32[]{:S(2)}) copy-start(f32[1024,512]{1,0:T(8,128)S(1)} %fusion.27) | copy-start | bytes 6291460 | tf_op jit(solution)/shard_map/while
  239.5 37.8 %collective-permute-start = (bf16[1024,512]{1,0:T(8,128)(2,1)S(1)}, bf16[1024,512]{1,0:T(8,128)(2,1)}, u32[]{:S(2)}, u32[]{:S(2)}) collective-permute-start(bf16[1024,512]{1,0:T(8,128)(2,1)S(1)} %copy.21), channel_id=1, source_target_pairs={{1,0},{2,1},{3,2},{4,3},{5,4},{6,5},{7,6},{8,7},{9,8},{10,9},{11,1... | collective-permute-start | bytes 3145736 | tf_op jit(solution)/shard_map/while/body/eval_jaxpr/ppermute | solution.py:10
  240.9 40.1 %collective-permute-start.2 = (bf16[1024,512]{1,0:T(8,128)(2,1)S(1)}, bf16[1024,512]{1,0:T(8,128)(2,1)S(1)}, u32[]{:S(2)}, u32[]{:S(2)}) collective-permute-start(bf16[1024,512]{1,0:T(8,128)(2,1)S(1)} %copy.22), channel_id=1, source_target_pairs={{16,0},{32,16},{48,32},{64,48},{80,64},{96,80},{112,96},{0,112},{1... | collective-permute-start | bytes 3145736 | tf_op jit(solution)/shard_map/while/body/eval_jaxpr/ppermute | solution.py:10
  277.3 16.0 %collective-permute-start.1 = (bf16[1024,512]{1,0:T(8,128)(2,1)}, bf16[1024,512]{1,0:T(8,128)(2,1)}, u32[]{:S(2)}, u32[]{:S(2)}) collective-permute-start(bf16[1024,512]{1,0:T(8,128)(2,1)} %collective-permute-done), channel_id=1, source_target_pairs={{1,0},{2,1},{3,2},{4,3},{5,4},{6,5},{7,6},{8,7},{9,8},{10,9},{11,1... | collective-permute-start | bytes 3145736 | tf_op jit(solution)/shard_map/while/body/eval_jaxpr/ppermute | solution.py:10
  277.3 1.6 copy-start
  281.0 12.3 %copy-start.1 = (f32[1024,512]{1,0:T(8,128)}, f32[1024,512]{1,0:T(8,128)S(1)}, u32[]{:S(2)}) copy-start(f32[1024,512]{1,0:T(8,128)S(1)} %fusion.27) | copy-start | bytes 6291460 | tf_op jit(solution)/shard_map/while
  294.6 38.3 %collective-permute-start = (bf16[1024,512]{1,0:T(8,128)(2,1)S(1)}, bf16[1024,512]{1,0:T(8,128)(2,1)}, u32[]{:S(2)}, u32[]{:S(2)}) collective-permute-start(bf16[1024,512]{1,0:T(8,128)(2,1)S(1)} %copy.21), channel_id=1, source_target_pairs={{1,0},{2,1},{3,2},{4,3},{5,4},{6,5},{7,6},{8,7},{9,8},{10,9},{11,1... | collective-permute-start | bytes 3145736 | tf_op jit(solution)/shard_map/while/body/eval_jaxpr/ppermute | solution.py:10
  295.2 41.4 %collective-permute-start.2 = (bf16[1024,512]{1,0:T(8,128)(2,1)S(1)}, bf16[1024,512]{1,0:T(8,128)(2,1)S(1)}, u32[]{:S(2)}, u32[]{:S(2)}) collective-permute-start(bf16[1024,512]{1,0:T(8,128)(2,1)S(1)} %copy.22), channel_id=1, source_target_pairs={{16,0},{32,16},{48,32},{64,48},{80,64},{96,80},{112,96},{0,112},{1... | collective-permute-start | bytes 3145736 | tf_op jit(solution)/shard_map/while/body/eval_jaxpr/ppermute | solution.py:10
  332.9 16.0 %collective-permute-start.1 = (bf16[1024,512]{1,0:T(8,128)(2,1)}, bf16[1024,512]{1,0:T(8,128)(2,1)}, u32[]{:S(2)}, u32[]{:S(2)}) collective-permute-start(bf16[1024,512]{1,0:T(8,128)(2,1)} %collective-permute-done), channel_id=1, source_target_pairs={{1,0},{2,1},{3,2},{4,3},{5,4},{6,5},{7,6},{8,7},{9,8},{10,9},{11,1... | collective-permute-start | bytes 3145736 | tf_op jit(solution)/shard_map/while/body/eval_jaxpr/ppermute | solution.py:10
  336.6 12.4 %copy-start.1 = (f32[1024,512]{1,0:T(8,128)}, f32[1024,512]{1,0:T(8,128)S(1)}, u32[]{:S(2)}) copy-start(f32[1024,512]{1,0:T(8,128)S(1)} %fusion.27) | copy-start | bytes 6291460 | tf_op jit(solution)/shard_map/while
  350.1 37.9 %collective-permute-start = (bf16[1024,512]{1,0:T(8,128)(2,1)S(1)}, bf16[1024,512]{1,0:T(8,128)(2,1)}, u32[]{:S(2)}, u32[]{:S(2)}) collective-permute-start(bf16[1024,512]{1,0:T(8,128)(2,1)S(1)} %copy.21), channel_id=1, source_target_pairs={{1,0},{2,1},{3,2},{4,3},{5,4},{6,5},{7,6},{8,7},{9,8},{10,9},{11,1... | collective-permute-start | bytes 3145736 | tf_op jit(solution)/shard_map/while/body/eval_jaxpr/ppermute | solution.py:10
  351.0 40.8 %collective-permute-start.2 = (bf16[1024,512]{1,0:T(8,128)(2,1)S(1)}, bf16[1024,512]{1,0:T(8,128)(2,1)S(1)}, u32[]{:S(2)}, u32[]{:S(2)}) collective-permute-start(bf16[1024,512]{1,0:T(8,128)(2,1)S(1)} %copy.22), channel_id=1, source_target_pairs={{16,0},{32,16},{48,32},{64,48},{80,64},{96,80},{112,96},{0,112},{1... | collective-permute-start | bytes 3145736 | tf_op jit(solution)/shard_map/while/body/eval_jaxpr/ppermute | solution.py:10
  388.1 16.0 %collective-permute-start.1 = (bf16[1024,512]{1,0:T(8,128)(2,1)}, bf16[1024,512]{1,0:T(8,128)(2,1)}, u32[]{:S(2)}, u32[]{:S(2)}) collective-permute-start(bf16[1024,512]{1,0:T(8,128)(2,1)} %collective-permute-done), channel_id=1, source_target_pairs={{1,0},{2,1},{3,2},{4,3},{5,4},{6,5},{7,6},{8,7},{9,8},{10,9},{11,1... | collective-permute-start | bytes 3145736 | tf_op jit(solution)/shard_map/while/body/eval_jaxpr/ppermute | solution.py:10
  388.1 1.6 copy-start
  391.8 12.4 %copy-start.1 = (f32[1024,512]{1,0:T(8,128)}, f32[1024,512]{1,0:T(8,128)S(1)}, u32[]{:S(2)}) copy-start(f32[1024,512]{1,0:T(8,128)S(1)} %fusion.27) | copy-start | bytes 6291460 | tf_op jit(solution)/shard_map/while
  405.3 38.3 %collective-permute-start = (bf16[1024,512]{1,0:T(8,128)(2,1)S(1)}, bf16[1024,512]{1,0:T(8,128)(2,1)}, u32[]{:S(2)}, u32[]{:S(2)}) collective-permute-start(bf16[1024,512]{1,0:T(8,128)(2,1)S(1)} %copy.21), channel_id=1, source_target_pairs={{1,0},{2,1},{3,2},{4,3},{5,4},{6,5},{7,6},{8,7},{9,8},{10,9},{11,1... | collective-permute-start | bytes 3145736 | tf_op jit(solution)/shard_map/while/body/eval_jaxpr/ppermute | solution.py:10
  405.4 41.9 %collective-permute-start.2 = (bf16[1024,512]{1,0:T(8,128)(2,1)S(1)}, bf16[1024,512]{1,0:T(8,128)(2,1)S(1)}, u32[]{:S(2)}, u32[]{:S(2)}) collective-permute-start(bf16[1024,512]{1,0:T(8,128)(2,1)S(1)} %copy.22), channel_id=1, source_target_pairs={{16,0},{32,16},{48,32},{64,48},{80,64},{96,80},{112,96},{0,112},{1... | collective-permute-start | bytes 3145736 | tf_op jit(solution)/shard_map/while/body/eval_jaxpr/ppermute | solution.py:10
  443.6 16.0 %collective-permute-start.1 = (bf16[1024,512]{1,0:T(8,128)(2,1)}, bf16[1024,512]{1,0:T(8,128)(2,1)}, u32[]{:S(2)}, u32[]{:S(2)}) collective-permute-start(bf16[1024,512]{1,0:T(8,128)(2,1)} %collective-permute-done), channel_id=1, source_target_pairs={{1,0},{2,1},{3,2},{4,3},{5,4},{6,5},{7,6},{8,7},{9,8},{10,9},{11,1... | collective-permute-start | bytes 3145736 | tf_op jit(solution)/shard_map/while/body/eval_jaxpr/ppermute | solution.py:10
  443.6 1.6 copy-start
  447.3 12.4 %copy-start.1 = (f32[1024,512]{1,0:T(8,128)}, f32[1024,512]{1,0:T(8,128)S(1)}, u32[]{:S(2)}) copy-start(f32[1024,512]{1,0:T(8,128)S(1)} %fusion.27) | copy-start | bytes 6291460 | tf_op jit(solution)/shard_map/while
  460.9 36.7 %collective-permute-start = (bf16[1024,512]{1,0:T(8,128)(2,1)S(1)}, bf16[1024,512]{1,0:T(8,128)(2,1)}, u32[]{:S(2)}, u32[]{:S(2)}) collective-permute-start(bf16[1024,512]{1,0:T(8,128)(2,1)S(1)} %copy.21), channel_id=1, source_target_pairs={{1,0},{2,1},{3,2},{4,3},{5,4},{6,5},{7,6},{8,7},{9,8},{10,9},{11,1... | collective-permute-start | bytes 3145736 | tf_op jit(solution)/shard_map/while/body/eval_jaxpr/ppermute | solution.py:10
  461.0 40.3 %collective-permute-start.2 = (bf16[1024,512]{1,0:T(8,128)(2,1)S(1)}, bf16[1024,512]{1,0:T(8,128)(2,1)S(1)}, u32[]{:S(2)}, u32[]{:S(2)}) collective-permute-start(bf16[1024,512]{1,0:T(8,128)(2,1)S(1)} %copy.22), channel_id=1, source_target_pairs={{16,0},{32,16},{48,32},{64,48},{80,64},{96,80},{112,96},{0,112},{1... | collective-permute-start | bytes 3145736 | tf_op jit(solution)/shard_map/while/body/eval_jaxpr/ppermute | solution.py:10
  497.6 16.0 %collective-permute-start.1 = (bf16[1024,512]{1,0:T(8,128)(2,1)}, bf16[1024,512]{1,0:T(8,128)(2,1)}, u32[]{:S(2)}, u32[]{:S(2)}) collective-permute-start(bf16[1024,512]{1,0:T(8,128)(2,1)} %collective-permute-done), channel_id=1, source_target_pairs={{1,0},{2,1},{3,2},{4,3},{5,4},{6,5},{7,6},{8,7},{9,8},{10,9},{11,1... | collective-permute-start | bytes 3145736 | tf_op jit(solution)/shard_map/while/body/eval_jaxpr/ppermute | solution.py:10
  497.6 1.6 copy-start
  501.3 12.4 %copy-start.1 = (f32[1024,512]{1,0:T(8,128)}, f32[1024,512]{1,0:T(8,128)S(1)}, u32[]{:S(2)}) copy-start(f32[1024,512]{1,0:T(8,128)S(1)} %fusion.27) | copy-start | bytes 6291460 | tf_op jit(solution)/shard_map/while
  513.7 15.9 %collective-permute-start.11 = (bf16[1024,512]{1,0:T(8,128)(2,1)}, bf16[1024,512]{1,0:T(8,128)(2,1)S(1)}, u32[]{:S(2)}, u32[]{:S(2)}) collective-permute-start(bf16[1024,512]{1,0:T(8,128)(2,1)} %get-tuple-element.30), channel_id=1, source_target_pairs={{1,0},{2,1},{3,2},{4,3},{5,4},{6,5},{7,6},{8,7},{9,8},{10,9},{11,1... | collective-permute-start | bytes 3145736 | tf_op jit(solution)/shard_map/ppermute | solution.py:10
  516.5 14.4 %copy-start.2 = (f32[1024,512]{1,0:T(8,128)S(1)}, f32[1024,512]{1,0:T(8,128)}, u32[]{:S(2)}) copy-start(f32[1024,512]{1,0:T(8,128)} %get-tuple-element.29) | copy-start | bytes 6291460
  (1 other events, 1.6 us)
where the time goes:
time: 535 us; the launch traced here: 533 us
  waiting for transfers between devices  447 us (84%)
  starting transfers between devices  29.6 us (6%)
  matrix products  23.1 us (4%)
  local copies, waits for them, and re-layouts  22.9 us (4%)
  other arithmetic  9.6 us (2%)
    ppermute x30, waiting for transfers between devices, from_behind(): return lax.ppermute(block, axis, route)  447 us
    ppermute x30, starting transfers between devices, from_behind(): return lax.ppermute(block, axis, route)  29.6 us
    dot_general x16, matrix products, run_group(): jnp.dot(left_now, panel_now, preferred_element_type=jnp.float32)  23.1 us
    while x42, local copies, waits for them, and re-layouts  15.3 us
  transfers between devices with their start and end apart: 30, of which 23 were waited for; matrix products, arithmetic and copies ran while one was open for 6% of the time, Pallas kernels for 0%

commit v1 on v0

v1 whole, which is shorter than its diff:
```python
import jax
import jax.numpy as jnp
from jax import lax
from jax.experimental import pallas as pl
from jax.experimental.pallas import tpu as pltpu
from jax.sharding import PartitionSpec as P

MESH = pl.DeviceIdType.MESH
BLOCK = 128
ROWS = 1024
COLS = 512
PIECES = 4
PIECE = ROWS // PIECES
HALF = PIECES // 2

OWN, LEFT, RIGHT, FAR, P_OWN, P_LEFT, P_RIGHT, P_FAR = range(8)
RING_STEP = (0, 3, 1, 2, 0, 3, 1, 2)

FROM_LEFT = ((0, 160), (160, 160))
FROM_PLANE = ((320, 192), (512, 192))
FROM_RIGHT = ((704, 160), (864, 160))
FAR_PARTS = FROM_LEFT + FROM_PLANE + FROM_RIGHT
N_PARTS = 7 * PIECES + len(FAR_PARTS)


def pieces_of(origin):
    if origin == P_FAR:
        return FAR_PARTS
    return tuple((i * PIECE, PIECE) for i in range(PIECES))


def kernel(
    left_in, right_in, a_pat, b_pat, keep, out,
    a_all, b_all, total, load_sem, a_send, a_recv, b_send, b_recv, c_send, c_recv,
):
    row = lax.axis_index("row")
    col = lax.axis_index("col")
    x = row // 2
    y_lo = row % 2
    z = col // 4
    y_hi = col // 2 % 2
    core = col % 2

    x_up = ((x + 1) % 4 * 2 + y_lo, col)
    x_down = ((x + 3) % 4 * 2 + y_lo, col)
    b_plane = (x * 2 + 1 - y_lo, col)
    z_up = (row, (z + 1) % 4 * 4 + col % 4)
    z_down = (row, (z + 3) % 4 * 4 + col % 4)
    a_plane = (row, z * 4 + (1 - y_hi) * 2 + core)
    sibling = (row, col // 2 * 2 + 1 - core)

    def a_chunk(origin):
        plane = y_hi if origin < P_OWN else 1 - y_hi
        return (z + RING_STEP[origin]) % 4 * 2 + plane

    def b_chunk(origin):
        plane = y_lo if origin < P_OWN else 1 - y_lo
        return (x + RING_STEP[origin]) % 4 * 2 + plane

    barrier = pltpu.get_barrier_semaphore()
    partners = (x_up, x_down, b_plane, z_up, z_down, a_plane, sibling)
    for partner in partners:
        pl.semaphore_signal(barrier, inc=1, device_id=partner, device_id_type=MESH)

    a_own, b_own = a_chunk(OWN), b_chunk(OWN)
    loads = []
    for i in range(PIECES):
        rows = pl.ds(i * PIECE, PIECE)
        for which, (source, held) in enumerate(
            ((right_in, b_all.at[b_own]), (left_in, a_all.at[a_own, core]))
        ):
            load = pltpu.make_async_copy(
                source.at[rows], held.at[rows], load_sem.at[which, i]
            )
            load.start()
            loads.append(load)

    def mask(held, pattern, i):
        for bi in range(i * PIECE // BLOCK, (i + 1) * PIECE // BLOCK):
            for bj in range(COLS // BLOCK):
                cells = (pl.ds(bi * BLOCK, BLOCK), pl.ds(bj * BLOCK, BLOCK))
                stored = jnp.full((BLOCK, BLOCK), pattern[bi, bj].astype(jnp.float32))
                held[cells] = held[cells] * stored.astype(jnp.bfloat16)

    sent = []

    class Stream:
        def __init__(self, slot_of, send_sem, recv_sem):
            self.slot_of, self.send_sem, self.recv_sem = slot_of, send_sem, recv_sem
            self.count = 0

        def send(self, origin, span, to, arrives_as, index):
            ref = self.slot_of(origin).at[pl.ds(*span)]
            copy = pltpu.make_async_remote_copy(
                src_ref=ref,
                dst_ref=ref,
                send_sem=self.send_sem.at[self.count],
                recv_sem=self.recv_sem.at[arrives_as * PIECES + index],
                device_id=to,
                device_id_type=MESH,
            )
            self.count += 1
            copy.start()
            sent.append(copy)

        def wait(self, origin, index):
            ref = self.slot_of(origin).at[pl.ds(*pieces_of(origin)[index])]
            pltpu.make_async_remote_copy(
                src_ref=ref,
                dst_ref=ref,
                send_sem=self.send_sem.at[0],
                recv_sem=self.recv_sem.at[origin * PIECES + index],
                device_id=sibling,
                device_id_type=MESH,
            ).wait_recv()

    a_stream = Stream(lambda o: a_all.at[a_chunk(o), core], a_send, a_recv)
    b_stream = Stream(lambda o: b_all.at[b_chunk(o)], b_send, b_recv)
    c_stream = Stream(lambda o: a_all.at[a_chunk(o), core], c_send, c_recv)
    c_wait = Stream(lambda o: a_all.at[a_chunk(o), 1 - core], c_send, c_recv)

    def share(origin, index):
        c_stream.send(origin, pieces_of(origin)[index], sibling, origin, index)

    a_links = (a_stream, z_up, z_down, a_plane)
    b_links = (b_stream, x_up, x_down, b_plane)

    def arrived(links, origin, index):
        stream = links[0]
        stream.wait(origin, index)
        if stream is a_stream:
            share(origin, index)

    def send_own(links, i):
        stream, up, down, plane = links
        span = pieces_of(OWN)[i]
        stream.send(OWN, span, up, LEFT, i)
        stream.send(OWN, span, down, RIGHT, i)
        stream.send(OWN, span, plane, P_OWN, i)
        if stream is a_stream:
            share(OWN, i)

    for i in range(PIECES):
        loads[2 * i].wait()
        mask(b_all.at[b_own], b_pat, i)
        loads[2 * i + 1].wait()
        mask(a_all.at[a_own, core], a_pat, i)
        if i == 0:
            pl.semaphore_wait(barrier, len(partners))
        send_own(b_links, i)
        send_own(a_links, i)

    def ring_step(links, i):
        stream, up, down, _ = links
        arrived(links, LEFT, i)
        if i < HALF:
            stream.send(LEFT, pieces_of(LEFT)[i], up, FAR, i)
        arrived(links, RIGHT, i)
        if i >= HALF:
            stream.send(RIGHT, pieces_of(RIGHT)[i], down, FAR, i)

    def plane_step(links, i):
        stream, up, down, _ = links
        arrived(links, P_OWN, i)
        span = pieces_of(P_OWN)[i]
        stream.send(P_OWN, span, up, P_LEFT, i)
        stream.send(P_OWN, span, down, P_RIGHT, i)

    both = (b_links, a_links)
    for i in range(PIECES):
        for links in both:
            ring_step(links, i)
        if i % 2 == 1:
            for links in both:
                plane_step(links, i // 2)
    for i, j in ((0, HALF), (HALF - 1, PIECES - 1)):
        for links in both:
            for index in dict.fromkeys((i, j)):
                arrived(links, FAR, index)
    n_left, n_plane = len(FROM_LEFT), len(FROM_PLANE)
    for links in both:
        stream, plane = links[0], links[3]
        for k, span in enumerate(FROM_PLANE):
            stream.send(FAR, span, plane, P_FAR, n_left + k)
    for i in range(HALF, PIECES):
        for links in both:
            plane_step(links, i)
    for i in range(PIECES):
        for links in both:
            arrived(links, P_LEFT, i)
            if i == HALF - 1:
                for k, span in enumerate(FROM_LEFT):
                    links[0].send(P_LEFT, span, links[1], P_FAR, k)
            arrived(links, P_RIGHT, i)
            if i == PIECES - 1:
                for k, span in enumerate(FROM_RIGHT):
                    links[0].send(P_RIGHT, span, links[2], P_FAR, n_left + n_plane + k)
    for index in range(len(FAR_PARTS)):
        for links in both:
            arrived(links, P_FAR, index)
    for origin in range(8):
        for index in range(len(pieces_of(origin))):
            c_wait.wait(origin, index)

    for chunk in range(8):

        def multiply(i, _, chunk=chunk):
            rows = pl.ds(pl.multiple_of(i * 256, 256), 256)
            product = jnp.dot(
                a_all[chunk, 0, rows, :], b_all[chunk, 0:COLS, :],
                preferred_element_type=jnp.float32,
            ) + jnp.dot(
                a_all[chunk, 1, rows, :], b_all[chunk, COLS:ROWS, :],
                preferred_element_type=jnp.float32,
            )
            if chunk == 0:
                total[rows, :] = product
            else:
                total[rows, :] += product
            return 0

        lax.fori_loop(0, ROWS // 256, multiply, 0)

    def finish(i, _):
        rows = pl.ds(pl.multiple_of(i * BLOCK, BLOCK), BLOCK)
        for j in range(COLS // BLOCK):
            cols = pl.ds(j * BLOCK, BLOCK)
            kept = jnp.full((BLOCK, BLOCK), keep[i, j].astype(jnp.float32))
            out[rows, cols] = (total[rows, cols] * kept).astype(jnp.bfloat16)
        return 0

    lax.fori_loop(0, ROWS // BLOCK, finish, 0)
    for copy in sent:
        copy.wait_send()


def on_device(left_blocks, right_blocks, a_pattern, b_pattern, keep_mask):
    n_sends = 64
    return pl.pallas_call(
        kernel,
        out_shape=jax.ShapeDtypeStruct((ROWS, COLS), jnp.bfloat16),
        in_specs=[pl.BlockSpec(memory_space=pl.ANY)] * 2
        + [pl.BlockSpec(memory_space=pltpu.SMEM)] * 3,
        out_specs=pl.BlockSpec(memory_space=pltpu.VMEM),
        scratch_shapes=[
            pltpu.VMEM((8, 2, ROWS, COLS), jnp.bfloat16),
            pltpu.VMEM((8, ROWS, COLS), jnp.bfloat16),
            pltpu.VMEM((ROWS, COLS), jnp.float32),
            pltpu.SemaphoreType.DMA((2, PIECES)),
            pltpu.SemaphoreType.DMA((n_sends,)),
            pltpu.SemaphoreType.DMA((N_PARTS,)),
            pltpu.SemaphoreType.DMA((n_sends,)),
            pltpu.SemaphoreType.DMA((N_PARTS,)),
            pltpu.SemaphoreType.DMA((n_sends,)),
            pltpu.SemaphoreType.DMA((N_PARTS,)),
        ],
        compiler_params=pltpu.CompilerParams(
            collective_id=0,
            has_side_effects=True,
            vmem_limit_bytes=48 * 1024 * 1024,
        ),
    )(left_blocks, right_blocks, a_pattern, b_pattern, keep_mask)


def solution(mesh):
    placed = (P("row", "col"),) * 5
    return jax.shard_map(
        on_device, mesh=mesh, in_specs=placed, out_specs=P("row", "col"), check_vma=False
    )
```

time: 535 us -> 97.3 us (0.18)
  waiting for transfers between devices: 447 us -> 0 us
  Pallas kernels: 0 us -> 92.1 us
  starting transfers between devices: 29.6 us -> 0 us
  matrix products: 23.1 us -> 0 us
  local copies, waits for them, and re-layouts: 22.9 us -> 4.96 us
  other arithmetic: 9.6 us -> 0 us
    ppermute x30 -> x0, waiting for transfers between devices: 447 us -> none  [from_behind(): return lax.ppermute(block, axis, route)]
    pallas_call x0 -> x1, Pallas kernels: none -> 92.1 us  [on_device(): pl.pallas_call(kernel, out_shape=jax.ShapeDtypeStruct((ROWS, COLS), jnp.b...]
    ppermute x30 -> x0, starting transfers between devices: 29.6 us -> none  [from_behind(): return lax.ppermute(block, axis, route)]
    dot_general x16 -> x0, matrix products: 23.1 us -> none  [run_group(): jnp.dot(left_now, panel_now, preferred_element_type=jnp.float32)]
    while x42 -> x0, local copies, waits for them, and re-layouts: 15.3 us -> none
    broadcast_in_dim x6 -> x0, local copies, waits for them, and re-layouts: 7.23 us -> none  [the longest x3 7.12 us: expand_blocks(): jnp.repeat(jnp.repeat(pattern_int, block_size, axis=0), block_size, axis=1)]
    select_n x7 -> x0, other arithmetic: 6.17 us -> none  [the longest x4 5.83 us: on_device(): jnp.where(left_amount // (1 << power) % 2 == 1, shifted, left_part)]
  transfers between devices with their start and end apart: 30 -> 0, of which waited for: 23 -> 0; matrix products, arithmetic and copies ran while one was open for 6% -> 0% of each run, Pallas kernels for 0% -> 0%
where the time goes in v1:
time: 97.3 us; the launch traced here: 97.1 us
  Pallas kernels  92.1 us (95%)
  local copies, waits for them, and re-layouts  4.96 us (5%)
    pallas_call x1, Pallas kernels, on_device(): pl.pallas_call(kernel, out_shape=jax.ShapeDtypeStruct((ROWS, COLS), jnp.b...  92.1 us
    unnamed x12, local copies, waits for them, and re-layouts  4.96 us

profile of v1, /device:TPU:1, one launch (start us, length us, event | category | flops | bytes accessed | tf_op | source)
XLA Modules:
  0.0 97.1 jit_solution(8173021259361308391)
XLA Ops:
  0.0 0.0 copy-start.2
  0.0 0.8 copy.6.a_pat
  0.8 0.0 copy-done.2
  0.8 0.0 copy-start.3
  0.8 0.1 copy.7.b_pat
  0.9 0.6 copy-done.3
  1.5 0.1 copy.8.keep
  1.5 0.0 copy-start
  1.5 1.2 %copy-done = bf16[1024,512]{1,0:T(8,128)(2,1)S(1)} copy-done((bf16[1024,512]{1,0:T(8,128)(2,1)S(1)}, bf16[1024,512]{1,0:T(8,128)(2,1)}, u32[]{:S(2)}) %copy-start) | copy-done | bytes 1048600
  2.8 0.0 copy-start.1
  2.8 1.2 %copy-done.1 = bf16[1024,512]{1,0:T(8,128)(2,1)S(1)} copy-done((bf16[1024,512]{1,0:T(8,128)(2,1)S(1)}, bf16[1024,512]{1,0:T(8,128)(2,1)}, u32[]{:S(2)}) %copy-start.1) | copy-done | bytes 1048600
  4.0 92.1 %shard_map.55 = bf16[1024,512]{1,0:T(8,128)(2,1)S(1)} custom-call(bf16[1024,512]{1,0:T(8,128)(2,1)S(1)} %copy-done, bf16[1024,512]{1,0:T(8,128)(2,1)S(1)} %copy-done.1, s32[8,4]{1,0:T(8,128)S(1)} %copy.6.a_pat, s32[8,4]{1,0:T(8,128)S(1)} %copy.7.b_pat, s32[8,4]{1,0:T(8,128)S(1)} %copy.8.keep), custom_call_target="tpu_custom_call" | custom-call | tf_op jit(solution)/shard_map/pallas_call | solution.py:239
  96.1 1.0 %copy.10 = bf16[1024,512]{1,0:T(8,128)(2,1)} copy(bf16[1024,512]{1,0:T(8,128)(2,1)S(1)} %shard_map.55) | data formatting | bytes 2097152
Async XLA Ops:
  0.0 0.8 copy-start.2
  0.8 0.7 copy-start.3
  1.5 1.2 %copy-start = (bf16[1024,512]{1,0:T(8,128)(2,1)S(1)}, bf16[1024,512]{1,0:T(8,128)(2,1)}, u32[]{:S(2)}) copy-start(bf16[1024,512]{1,0:T(8,128)(2,1)} %left_in.1) | copy-start | bytes 3145732
  2.8 1.2 %copy-start.1 = (bf16[1024,512]{1,0:T(8,128)(2,1)S(1)}, bf16[1024,512]{1,0:T(8,128)(2,1)}, u32[]{:S(2)}) copy-start(bf16[1024,512]{1,0:T(8,128)(2,1)} %right_in.1) | copy-start | bytes 3145732

commit v2 on v1

v2 whole, which is shorter than its diff:
```python
import jax
import jax.numpy as jnp
from jax import lax
from jax.experimental import pallas as pl
from jax.experimental.pallas import tpu as pltpu
from jax.sharding import PartitionSpec as P

MESH = pl.DeviceIdType.MESH
BLOCK = 128
ROWS = 1024
COLS = 512
PIECES = 4
PIECE = ROWS // PIECES
HALF = PIECES // 2

OWN, LEFT, RIGHT, FAR, P_OWN, P_LEFT, P_RIGHT, P_FAR = range(8)
RING_STEP = (0, 3, 1, 2, 0, 3, 1, 2)

A_FAR = ((0, 176), (176, 176), (352, 160), (512, 160), (672, 176), (848, 176))
B_FAR = ((0, 128), (128, 128), (256, 256), (512, 256), (768, 128), (896, 128))
PER_ORIGIN = 6


def kernel(
    left_in, right_in, a_pat_in, b_pat_in, keep_in, out,
    a_all, b_all, total, a_pat, b_pat, keep,
    load_sem, pat_sem, a_send, a_recv, b_send, b_recv, c_send, c_recv,
):
    row = lax.axis_index("row")
    col = lax.axis_index("col")
    x = row // 2
    y_lo = row % 2
    z = col // 4
    y_hi = col // 2 % 2
    core = col % 2

    x_up = ((x + 1) % 4 * 2 + y_lo, col)
    x_down = ((x + 3) % 4 * 2 + y_lo, col)
    b_plane = (x * 2 + 1 - y_lo, col)
    z_up = (row, (z + 1) % 4 * 4 + col % 4)
    z_down = (row, (z + 3) % 4 * 4 + col % 4)
    a_plane = (row, z * 4 + (1 - y_hi) * 2 + core)
    sibling = (row, col // 2 * 2 + 1 - core)

    def a_chunk(origin):
        plane = y_hi if origin < P_OWN else 1 - y_hi
        return (z + RING_STEP[origin]) % 4 * 2 + plane

    def b_chunk(origin):
        plane = y_lo if origin < P_OWN else 1 - y_lo
        return (x + RING_STEP[origin]) % 4 * 2 + plane

    barrier = pltpu.get_barrier_semaphore()
    partners = (x_up, x_down, b_plane, z_up, z_down, a_plane, sibling)
    for partner in partners:
        pl.semaphore_signal(barrier, inc=1, device_id=partner, device_id_type=MESH)

    a_own, b_own = a_chunk(OWN), b_chunk(OWN)
    patterns = [
        pltpu.make_async_copy(source, held, pat_sem.at[i])
        for i, (source, held) in enumerate(
            ((b_pat_in, b_pat), (a_pat_in, a_pat), (keep_in, keep))
        )
    ]
    for copy in patterns:
        copy.start()
    loads = []
    for i in range(PIECES):
        rows = pl.ds(i * PIECE, PIECE)
        for which, (source, held) in enumerate(
            ((right_in, b_all.at[b_own]), (left_in, a_all.at[a_own, core]))
        ):
            load = pltpu.make_async_copy(
                source.at[rows], held.at[rows], load_sem.at[which, i]
            )
            load.start()
            loads.append(load)

    def mask(held, pattern, i):
        for bi in range(i * PIECE // BLOCK, (i + 1) * PIECE // BLOCK):
            for bj in range(COLS // BLOCK):
                cells = (pl.ds(bi * BLOCK, BLOCK), pl.ds(bj * BLOCK, BLOCK))
                stored = jnp.full((BLOCK, BLOCK), pattern[bj, bi].astype(jnp.float32))
                held[cells] = held[cells] * stored.astype(jnp.bfloat16)

    sent = []

    class Stream:
        def __init__(self, slot_of, far, send_sem, recv_sem):
            self.slot_of, self.far = slot_of, far
            self.send_sem, self.recv_sem = send_sem, recv_sem
            self.count = 0

        def spans(self, origin):
            if origin == P_FAR:
                return self.far
            return tuple((i * PIECE, PIECE) for i in range(PIECES))

        def send(self, origin, span, to, arrives_as, index):
            ref = self.slot_of(origin).at[pl.ds(*span)]
            copy = pltpu.make_async_remote_copy(
                src_ref=ref,
                dst_ref=ref,
                send_sem=self.send_sem.at[self.count],
                recv_sem=self.recv_sem.at[arrives_as * PER_ORIGIN + index],
                device_id=to,
                device_id_type=MESH,
            )
            self.count += 1
            copy.start()
            sent.append(copy)

        def wait(self, origin, index):
            ref = self.slot_of(origin).at[pl.ds(*self.spans(origin)[index])]
            pltpu.make_async_remote_copy(
                src_ref=ref,
                dst_ref=ref,
                send_sem=self.send_sem.at[0],
                recv_sem=self.recv_sem.at[origin * PER_ORIGIN + index],
                device_id=sibling,
                device_id_type=MESH,
            ).wait_recv()

    a_stream = Stream(lambda o: a_all.at[a_chunk(o), core], A_FAR, a_send, a_recv)
    b_stream = Stream(lambda o: b_all.at[b_chunk(o)], B_FAR, b_send, b_recv)
    c_stream = Stream(lambda o: a_all.at[a_chunk(o), core], A_FAR, c_send, c_recv)
    c_wait = Stream(lambda o: a_all.at[a_chunk(o), 1 - core], A_FAR, c_send, c_recv)

    a_links = (a_stream, z_up, z_down, a_plane)
    b_links = (b_stream, x_up, x_down, b_plane)
    both = (b_links, a_links)

    def share(origin, index):
        c_stream.send(origin, a_stream.spans(origin)[index], sibling, origin, index)

    def arrived(links, origin, index):
        stream = links[0]
        stream.wait(origin, index)
        if stream is a_stream:
            share(origin, index)

    def shared(*origins):
        for origin in origins:
            for index in range(len(a_stream.spans(origin))):
                c_wait.wait(origin, index)

    def send_own(links, i):
        stream, up, down, plane = links
        span = stream.spans(OWN)[i]
        stream.send(OWN, span, up, LEFT, i)
        stream.send(OWN, span, down, RIGHT, i)
        stream.send(OWN, span, plane, P_OWN, i)
        if stream is a_stream:
            share(OWN, i)

    def ring_step(links, i):
        stream, up, down, _ = links
        arrived(links, LEFT, i)
        if i < HALF:
            stream.send(LEFT, stream.spans(LEFT)[i], up, FAR, i)
        arrived(links, RIGHT, i)
        if i >= HALF:
            stream.send(RIGHT, stream.spans(RIGHT)[i], down, FAR, i)

    def plane_step(links, i):
        stream, up, down, _ = links
        arrived(links, P_OWN, i)
        span = stream.spans(P_OWN)[i]
        stream.send(P_OWN, span, up, P_LEFT, i)
        stream.send(P_OWN, span, down, P_RIGHT, i)

    def partner_ring_step(links, i):
        stream, up, down, _ = links
        arrived(links, P_LEFT, i)
        if i == HALF - 1:
            for k in (0, 1):
                stream.send(P_LEFT, stream.far[k], up, P_FAR, k)
        arrived(links, P_RIGHT, i)
        if i == PIECES - 1:
            for k in (4, 5):
                stream.send(P_RIGHT, stream.far[k], down, P_FAR, k)

    def multiply(chunk, first=False):
        product = jnp.dot(
            a_all[chunk, 0], b_all[chunk, 0:COLS], preferred_element_type=jnp.float32
        ) + jnp.dot(
            a_all[chunk, 1], b_all[chunk, COLS:ROWS], preferred_element_type=jnp.float32
        )
        if first:
            total[...] = product
        else:
            total[...] += product

    meet = 1 - (y_hi + y_lo) % 2
    turn = (x + 4 - z) % 4
    odd = turn % 2

    def choose(if_meet, otherwise):
        return meet * if_meet + (1 - meet) * otherwise

    def partner_chunk(step):
        return (z + step) % 4 * 2 + 1 - y_hi

    early = (
        choose(a_chunk(OWN), b_chunk(P_OWN)),
        choose(a_chunk(FAR), a_chunk(P_OWN)),
    )
    middle = (
        choose(a_chunk(LEFT), b_chunk(P_LEFT)),
        choose(a_chunk(RIGHT), b_chunk(P_RIGHT)),
        choose(partner_chunk(1 - odd), a_chunk(P_LEFT)),
        choose(partner_chunk((1 - odd) * 3 + odd * turn), a_chunk(P_RIGHT)),
    )
    b_late = choose(partner_chunk(odd * (4 - turn)), b_chunk(P_FAR))
    a_late = a_chunk(P_FAR)

    for copy in patterns[:2]:
        copy.wait()
    for i in range(PIECES):
        loads[2 * i].wait()
        mask(b_all.at[b_own], b_pat, i)
        loads[2 * i + 1].wait()
        mask(a_all.at[a_own, core], a_pat, i)
        if i == 0:
            pl.semaphore_wait(barrier, len(partners))
        send_own(b_links, i)
        send_own(a_links, i)

    for i in range(PIECES):
        for links in both:
            ring_step(links, i)
        if i % 2 == 1:
            for links in both:
                plane_step(links, i // 2)
    for i, j in ((0, HALF), (HALF - 1, PIECES - 1)):
        for links in both:
            for index in dict.fromkeys((i, j)):
                arrived(links, FAR, index)
    for links in both:
        stream, plane = links[0], links[3]
        for k in (2, 3):
            stream.send(FAR, stream.far[k], plane, P_FAR, k)
    for i in range(HALF, PIECES):
        for links in both:
            plane_step(links, i)
    shared(OWN, LEFT, RIGHT, FAR, P_OWN)
    multiply(early[0], first=True)
    for links in both:
        partner_ring_step(links, 0)
    multiply(early[1])
    for i in range(1, PIECES):
        for links in both:
            partner_ring_step(links, i)
    shared(P_LEFT, P_RIGHT)
    for n, chunk in enumerate(middle):
        multiply(chunk)
        if n >= 2:
            arrived(a_links, P_FAR, n)
    for k in (2, 3, 0, 4, 1, 5):
        arrived(b_links, P_FAR, k)
        if k in (0, 4):
            arrived(a_links, P_FAR, k)
        first, rows = B_FAR[k]
        total[...] += jnp.dot(
            a_all[b_late, first // COLS, :, first % COLS : first % COLS + rows],
            b_all[b_late, first : first + rows],
            preferred_element_type=jnp.float32,
        )
    for k in (1, 5):
        arrived(a_links, P_FAR, k)
    for k in (2, 3, 0, 4, 1, 5):
        first, rows = A_FAR[k]
        cells = pl.ds(first, rows)
        c_wait.wait(P_FAR, k)
        total[cells] += jnp.dot(
            a_all[a_late, 0, cells], b_all[a_late, 0:COLS],
            preferred_element_type=jnp.float32,
        ) + jnp.dot(
            a_all[a_late, 1, cells], b_all[a_late, COLS:ROWS],
            preferred_element_type=jnp.float32,
        )

    patterns[2].wait()

    def finish(i, _):
        rows = pl.ds(pl.multiple_of(i * BLOCK, BLOCK), BLOCK)
        for j in range(COLS // BLOCK):
            cols = pl.ds(j * BLOCK, BLOCK)
            kept = jnp.full((BLOCK, BLOCK), keep[j, i].astype(jnp.float32))
            out[rows, cols] = (total[rows, cols] * kept).astype(jnp.bfloat16)
        return 0

    lax.fori_loop(0, ROWS // BLOCK, finish, 0)
    for copy in sent:
        copy.wait_send()


def on_device(left_blocks, right_blocks, a_pattern, b_pattern, keep_mask):
    n_sends = 64
    n_parts = 8 * PER_ORIGIN
    pattern = pltpu.SMEM(keep_mask.T.shape, jnp.int32)
    return pl.pallas_call(
        kernel,
        out_shape=jax.ShapeDtypeStruct((ROWS, COLS), jnp.bfloat16),
        in_specs=[pl.BlockSpec(memory_space=pltpu.HBM)] * 5,
        out_specs=pl.BlockSpec(memory_space=pltpu.VMEM),
        scratch_shapes=[
            pltpu.VMEM((8, 2, ROWS, COLS), jnp.bfloat16),
            pltpu.VMEM((8, ROWS, COLS), jnp.bfloat16),
            pltpu.VMEM((ROWS, COLS), jnp.float32),
            pattern,
            pattern,
            pattern,
            pltpu.SemaphoreType.DMA((2, PIECES)),
            pltpu.SemaphoreType.DMA((3,)),
            pltpu.SemaphoreType.DMA((n_sends,)),
            pltpu.SemaphoreType.DMA((n_parts,)),
            pltpu.SemaphoreType.DMA((n_sends,)),
            pltpu.SemaphoreType.DMA((n_parts,)),
            pltpu.SemaphoreType.DMA((n_sends,)),
            pltpu.SemaphoreType.DMA((n_parts,)),
        ],
        compiler_params=pltpu.CompilerParams(
            collective_id=0,
            has_side_effects=True,
            vmem_limit_bytes=40 * 1024 * 1024,
        ),
    )(*[pltpu.with_memory_space_constraint(v, pltpu.HBM) for v in (left_blocks, right_blocks, a_pattern.T, b_pattern.T, keep_mask.T)])


def solution(mesh):
    placed = (P("row", "col"),) * 5
    return jax.shard_map(
        on_device, mesh=mesh, in_specs=placed, out_specs=P("row", "col"), check_vma=False
    )
```

time: 97.3 us -> 80.8 us (0.83)
  Pallas kernels: 92.1 us -> 79.7 us
  local copies, waits for them, and re-layouts: 4.96 us -> 0.97 us
    pallas_call x1, Pallas kernels: 92.1 us -> 79.7 us  [on_device(): pl.pallas_call(kernel, out_shape=jax.ShapeDtypeStruct((ROWS, COLS), jnp.b...]
    unnamed x12 -> x1, local copies, waits for them, and re-layouts: 4.96 us -> 0.97 us
where the time goes in v2:
time: 80.8 us; the launch traced here: 80.7 us
  Pallas kernels  79.7 us (99%)
  local copies, waits for them, and re-layouts  0.97 us (1%)
    pallas_call x1, Pallas kernels, on_device(): pl.pallas_call(kernel, out_shape=jax.ShapeDtypeStruct((ROWS, COLS), jnp.b...  79.7 us

profile of v2, /device:TPU:1, one launch (start us, length us, event | category | flops | bytes accessed | tf_op | source)
XLA Modules:
  0.0 80.7 jit_solution(5119509933087261187)
XLA Ops:
  0.0 79.7 %shard_map.55 = bf16[1024,512]{1,0:T(8,128)(2,1)S(1)} custom-call(bf16[1024,512]{1,0:T(8,128)(2,1)} %left_in.1, bf16[1024,512]{1,0:T(8,128)(2,1)} %right_in.1, s32[4,8]{1,0:T(4,128)} %bitcast.3, s32[4,8]{1,0:T(4,128)} %bitcast.4, s32[4,8]{1,0:T(4,128)} %bitcast.5), custom_call_target="tpu_custom_call" | custom-call | tf_op jit(solution)/shard_map/pallas_call | solution.py:302
  79.7 1.0 %copy.7 = bf16[1024,512]{1,0:T(8,128)(2,1)} copy(bf16[1024,512]{1,0:T(8,128)(2,1)S(1)} %shard_map.55) | data formatting | bytes 2097152

commit v3 on v2

--- a/solution.py
+++ b/solution.py
@@ -16,9 +16,17 @@
 OWN, LEFT, RIGHT, FAR, P_OWN, P_LEFT, P_RIGHT, P_FAR = range(8)
 RING_STEP = (0, 3, 1, 2, 0, 3, 1, 2)
 
-A_FAR = ((0, 176), (176, 176), (352, 160), (512, 160), (672, 176), (848, 176))
-B_FAR = ((0, 128), (128, 128), (256, 256), (512, 256), (768, 128), (896, 128))
-PER_ORIGIN = 6
+A_FAR = (
+    ((0, 128), (128, 128)),
+    ((256, 128), (384, 128)),
+    ((512, 256), (768, 256)),
+)
+B_FAR = (
+    ((256, 96), (0, 128), (128, 128)),
+    ((352, 160), (512, 128), (640, 64)),
+    ((704, 64), (768, 256)),
+)
+PER_ORIGIN = 8
 
 
 def kernel(
@@ -87,7 +95,9 @@
 
     class Stream:
         def __init__(self, slot_of, far, send_sem, recv_sem):
-            self.slot_of, self.far = slot_of, far
+            self.slot_of, self.far = slot_of, far[0] + far[1] + far[2]
+            self.n_up, self.n_down = len(far[0]), len(far[1])
+            self.forwarded = 0
             self.send_sem, self.recv_sem = send_sem, recv_sem
             self.count = 0
 
@@ -169,16 +179,26 @@
         stream.send(P_OWN, span, up, P_LEFT, i)
         stream.send(P_OWN, span, down, P_RIGHT, i)
 
+    def forward(links, origin, to, first, stop, i):
+        stream = links[0]
+        covered = [span[0] + span[1] <= (i + 1) * PIECE for span in stream.far[first:stop]]
+        before = [span[0] + span[1] <= i * PIECE for span in stream.far[first:stop]]
+        if all(covered) and not all(before):
+            for k in range(first, stop):
+                stream.send(origin, stream.far[k], to, P_FAR, k)
+
     def partner_ring_step(links, i):
         stream, up, down, _ = links
+        n_up, n_down = stream.n_up, stream.n_down
         arrived(links, P_LEFT, i)
-        if i == HALF - 1:
-            for k in (0, 1):
-                stream.send(P_LEFT, stream.far[k], up, P_FAR, k)
+        forward(links, P_LEFT, up, 0, n_up, i)
         arrived(links, P_RIGHT, i)
-        if i == PIECES - 1:
-            for k in (4, 5):
-                stream.send(P_RIGHT, stream.far[k], down, P_FAR, k)
+        forward(links, P_RIGHT, down, n_up, n_up + n_down, i)
+
+    def plane_far(links):
+        stream, plane = links[0], links[3]
+        for k in range(stream.n_up + stream.n_down, len(stream.far)):
+            stream.send(FAR, stream.far[k], plane, P_FAR, k)
 
     def multiply(chunk, first=False):
         product = jnp.dot(
@@ -191,9 +211,27 @@
         else:
             total[...] += product
 
+    def add_depth(chunk, first, rows):
+        total[...] += jnp.dot(
+            a_all[chunk, first // COLS, :, first % COLS : first % COLS + rows],
+            b_all[chunk, first : first + rows],
+            preferred_element_type=jnp.float32,
+        )
+
+    def add_rows(chunk, first, rows):
+        cells = pl.ds(first, rows)
+        total[cells] += jnp.dot(
+            a_all[chunk, 0, cells], b_all[chunk, 0:COLS],
+            preferred_element_type=jnp.float32,
+        ) + jnp.dot(
+            a_all[chunk, 1, cells], b_all[chunk, COLS:ROWS],
+            preferred_element_type=jnp.float32,
+        )
+
     meet = 1 - (y_hi + y_lo) % 2
     turn = (x + 4 - z) % 4
     odd = turn % 2
+    turned = (turn + 3) // 4
 
     def choose(if_meet, otherwise):
         return meet * if_meet + (1 - meet) * otherwise
@@ -211,74 +249,70 @@
         choose(partner_chunk(1 - odd), a_chunk(P_LEFT)),
         choose(partner_chunk((1 - odd) * 3 + odd * turn), a_chunk(P_RIGHT)),
     )
-    b_late = choose(partner_chunk(odd * (4 - turn)), b_chunk(P_FAR))
-    a_late = a_chunk(P_FAR)
+    a_late = choose(partner_chunk(2 * turned), a_chunk(P_FAR))
+    b_late = b_chunk(P_FAR)
 
     for copy in patterns[:2]:
         copy.wait()
     for i in range(PIECES):
         loads[2 * i].wait()
         mask(b_all.at[b_own], b_pat, i)
-        loads[2 * i + 1].wait()
-        mask(a_all.at[a_own, core], a_pat, i)
         if i == 0:
             pl.semaphore_wait(barrier, len(partners))
         send_own(b_links, i)
+        loads[2 * i + 1].wait()
+        mask(a_all.at[a_own, core], a_pat, i)
         send_own(a_links, i)
 
     for i in range(PIECES):
         for links in both:
             ring_step(links, i)
-        if i % 2 == 1:
-            for links in both:
-                plane_step(links, i // 2)
+    for i in range(PIECES - 1):
+        for links in both:
+            plane_step(links, i)
     for i, j in ((0, HALF), (HALF - 1, PIECES - 1)):
         for links in both:
             for index in dict.fromkeys((i, j)):
                 arrived(links, FAR, index)
+    for links in both[::-1]:
+        plane_far(links)
     for links in both:
-        stream, plane = links[0], links[3]
-        for k in (2, 3):
-            stream.send(FAR, stream.far[k], plane, P_FAR, k)
-    for i in range(HALF, PIECES):
-        for links in both:
-            plane_step(links, i)
+        plane_step(links, PIECES - 1)
     shared(OWN, LEFT, RIGHT, FAR, P_OWN)
     multiply(early[0], first=True)
     for links in both:
         partner_ring_step(links, 0)
     multiply(early[1])
-    for i in range(1, PIECES):
+    for links in both:
+        partner_ring_step(links, 1)
+    add_depth(middle[0], 0, COLS)
+    add_depth(middle[1], 0, COLS)
+    for i in range(HALF, PIECES):
         for links in both:
             partner_ring_step(links, i)
     shared(P_LEFT, P_RIGHT)
-    for n, chunk in enumerate(middle):
-        multiply(chunk)
-        if n >= 2:
-            arrived(a_links, P_FAR, n)
-    for k in (2, 3, 0, 4, 1, 5):
+    add_depth(middle[0], COLS, COLS)
+    add_depth(middle[1], COLS, COLS)
+    multiply(middle[2])
+    for k in (4, 5):
+        arrived(a_links, P_FAR, k)
+    for k in (0, 2):
+        arrived(a_links, P_FAR, k)
+    multiply(middle[3])
+    for k in (1, 3):
+        arrived(a_links, P_FAR, k)
+    for k in (4, 5):
+        c_wait.wait(P_FAR, k)
+    add_rows(a_late, 512, 512)
+    for k in range(4):
+        c_wait.wait(P_FAR, k)
+    add_rows(a_late, 0, 512)
+    for k in (0, 3, 1, 2):
         arrived(b_links, P_FAR, k)
-        if k in (0, 4):
-            arrived(a_links, P_FAR, k)
-        first, rows = B_FAR[k]
-        total[...] += jnp.dot(
-            a_all[b_late, first // COLS, :, first % COLS : first % COLS + rows],
-            b_all[b_late, first : first + rows],
-            preferred_element_type=jnp.float32,
-        )
-    for k in (1, 5):
-        arrived(a_links, P_FAR, k)
-    for k in (2, 3, 0, 4, 1, 5):
-        first, rows = A_FAR[k]
-        cells = pl.ds(first, rows)
-        c_wait.wait(P_FAR, k)
-        total[cells] += jnp.dot(
-            a_all[a_late, 0, cells], b_all[a_late, 0:COLS],
-            preferred_element_type=jnp.float32,
-        ) + jnp.dot(
-            a_all[a_late, 1, cells], b_all[a_late, COLS:ROWS],
-            preferred_element_type=jnp.float32,
-        )
+    add_depth(b_late, 0, 512)
+    for k in (4, 5, 6, 7):
+        arrived(b_links, P_FAR, k)
+    add_depth(b_late, 512, 512)
 
     patterns[2].wait()
 

time: 80.8 us -> 78.9 us (0.976)
  Pallas kernels: 79.7 us -> 77.8 us
    pallas_call x1, Pallas kernels: 79.7 us -> 77.8 us  [on_device(): pl.pallas_call(kernel, out_shape=jax.ShapeDtypeStruct((ROWS, COLS), jnp.b...]
where the time goes in v3:
time: 78.9 us; the launch traced here: 78.8 us
  Pallas kernels  77.8 us (99%)
  local copies, waits for them, and re-layouts  0.97 us (1%)
    pallas_call x1, Pallas kernels, on_device(): pl.pallas_call(kernel, out_shape=jax.ShapeDtypeStruct((ROWS, COLS), jnp.b...  77.8 us

profile of v3, /device:TPU:1, one launch (start us, length us, event | category | flops | bytes accessed | tf_op | source)
XLA Modules:
  0.0 78.8 jit_solution(4425432149646702535)
XLA Ops:
  0.0 77.8 %shard_map.55 = bf16[1024,512]{1,0:T(8,128)(2,1)S(1)} custom-call(bf16[1024,512]{1,0:T(8,128)(2,1)} %left_in.1, bf16[1024,512]{1,0:T(8,128)(2,1)} %right_in.1, s32[4,8]{1,0:T(4,128)} %bitcast.3, s32[4,8]{1,0:T(4,128)} %bitcast.4, s32[4,8]{1,0:T(4,128)} %bitcast.5), custom_call_target="tpu_custom_call" | custom-call | tf_op jit(solution)/shard_map/pallas_call | solution.py:336
  77.8 1.0 %copy.7 = bf16[1024,512]{1,0:T(8,128)(2,1)} copy(bf16[1024,512]{1,0:T(8,128)(2,1)S(1)} %shard_map.55) | data formatting | bytes 2097152

commit v4 on v3

--- a/solution.py
+++ b/solution.py
@@ -17,16 +17,17 @@
 RING_STEP = (0, 3, 1, 2, 0, 3, 1, 2)
 
 A_FAR = (
-    ((0, 128), (128, 128)),
-    ((256, 128), (384, 128)),
-    ((512, 256), (768, 256)),
+    ((0, 112), (112, 128)),
+    ((368, 112), (240, 128)),
+    ((480, 272), (752, 272)),
 )
 B_FAR = (
-    ((256, 96), (0, 128), (128, 128)),
+    ((128, 224), (0, 128)),
     ((352, 160), (512, 128), (640, 64)),
-    ((704, 64), (768, 256)),
+    ((768, 256), (704, 64)),
 )
 PER_ORIGIN = 8
+ALL = (0, ROWS)
 
 
 def kernel(
@@ -154,6 +155,10 @@
             for index in range(len(a_stream.spans(origin))):
                 c_wait.wait(origin, index)
 
+    def shared_span(origin, *indices):
+        for index in indices:
+            c_wait.wait(origin, index)
+
     def send_own(links, i):
         stream, up, down, plane = links
         span = stream.spans(OWN)[i]
@@ -200,33 +205,41 @@
         for k in range(stream.n_up + stream.n_down, len(stream.far)):
             stream.send(FAR, stream.far[k], plane, P_FAR, k)
 
-    def multiply(chunk, first=False):
-        product = jnp.dot(
-            a_all[chunk, 0], b_all[chunk, 0:COLS], preferred_element_type=jnp.float32
-        ) + jnp.dot(
-            a_all[chunk, 1], b_all[chunk, COLS:ROWS], preferred_element_type=jnp.float32
-        )
-        if first:
-            total[...] = product
-        else:
-            total[...] += product
-
-    def add_depth(chunk, first, rows):
-        total[...] += jnp.dot(
-            a_all[chunk, first // COLS, :, first % COLS : first % COLS + rows],
-            b_all[chunk, first : first + rows],
+    def part_of(chunk, rows, depth):
+        cells = pl.ds(*rows)
+        first, count = depth
+        half, start = first // COLS, first % COLS
+        return jnp.dot(
+            a_all[chunk, half, cells, start : start + count],
+            b_all[chunk, first : first + count],
             preferred_element_type=jnp.float32,
         )
 
-    def add_rows(chunk, first, rows):
-        cells = pl.ds(first, rows)
-        total[cells] += jnp.dot(
+    def add(chunk, rows, depth):
+        total[pl.ds(*rows)] += part_of(chunk, rows, depth)
+
+    def product_of(chunk, rows):
+        cells = pl.ds(*rows)
+        return jnp.dot(
             a_all[chunk, 0, cells], b_all[chunk, 0:COLS],
             preferred_element_type=jnp.float32,
         ) + jnp.dot(
             a_all[chunk, 1, cells], b_all[chunk, COLS:ROWS],
             preferred_element_type=jnp.float32,
         )
+
+    def finish(rows, added):
+        first, count = rows
+        result = total[pl.ds(*rows)] + added
+        for bi in range(count // BLOCK):
+            for bj in range(COLS // BLOCK):
+                kept = keep[bj, first // BLOCK + bi].astype(jnp.float32)
+                block = result[
+                    bi * BLOCK : (bi + 1) * BLOCK, bj * BLOCK : (bj + 1) * BLOCK
+                ]
+                out[
+                    pl.ds(first + bi * BLOCK, BLOCK), pl.ds(bj * BLOCK, BLOCK)
+                ] = (block * kept).astype(jnp.bfloat16)
 
     meet = 1 - (y_hi + y_lo) % 2
     turn = (x + 4 - z) % 4
@@ -279,53 +292,62 @@
     for links in both:
         plane_step(links, PIECES - 1)
     shared(OWN, LEFT, RIGHT, FAR, P_OWN)
-    multiply(early[0], first=True)
+    total[...] = product_of(early[0], ALL)
     for links in both:
         partner_ring_step(links, 0)
-    multiply(early[1])
+    total[...] += product_of(early[1], ALL)
     for links in both:
         partner_ring_step(links, 1)
-    add_depth(middle[0], 0, COLS)
-    add_depth(middle[1], 0, COLS)
-    for i in range(HALF, PIECES):
-        for links in both:
-            partner_ring_step(links, i)
-    shared(P_LEFT, P_RIGHT)
-    add_depth(middle[0], COLS, COLS)
-    add_depth(middle[1], COLS, COLS)
-    multiply(middle[2])
+    add(middle[0], ALL, (0, 512))
+    add(middle[1], ALL, (0, 512))
+    shared_span(P_LEFT, 0, 1)
+    shared_span(P_RIGHT, 0, 1)
+    add(middle[2], (0, 512), (0, 512))
+    add(middle[3], (0, 512), (0, 512))
+    for links in both:
+        partner_ring_step(links, 2)
+    add(middle[0], ALL, (512, 256))
+    add(middle[1], ALL, (512, 256))
+    for links in both:
+        partner_ring_step(links, 3)
+    add(middle[0], ALL, (768, 256))
+    add(middle[1], ALL, (768, 256))
+    shared_span(P_LEFT, 2, 3)
+    shared_span(P_RIGHT, 2, 3)
+    add(middle[2], (512, 512), (0, 512))
+    add(middle[3], (512, 512), (0, 512))
+    ringed = list(sent)
     for k in (4, 5):
         arrived(a_links, P_FAR, k)
+    add(middle[2], ALL, (512, 512))
     for k in (0, 2):
         arrived(a_links, P_FAR, k)
-    multiply(middle[3])
+    add(middle[3], ALL, (512, 512))
+    for copy in ringed:
+        copy.wait_send()
     for k in (1, 3):
         arrived(a_links, P_FAR, k)
-    for k in (4, 5):
-        c_wait.wait(P_FAR, k)
-    add_rows(a_late, 512, 512)
-    for k in range(4):
-        c_wait.wait(P_FAR, k)
-    add_rows(a_late, 0, 512)
-    for k in (0, 3, 1, 2):
+    shared_span(P_FAR, 2, 4, 5)
+    total[pl.ds(368, 656)] += product_of(a_late, (368, 656))
+    for k in (0, 2):
         arrived(b_links, P_FAR, k)
-    add_depth(b_late, 0, 512)
-    for k in (4, 5, 6, 7):
+    add(b_late, (384, 640), (128, 384))
+    for k in (3, 5):
         arrived(b_links, P_FAR, k)
-    add_depth(b_late, 512, 512)
-
+    total[pl.ds(384, 640)] += part_of(b_late, (384, 640), (512, 128)) + part_of(
+        b_late, (384, 640), (768, 256)
+    )
     patterns[2].wait()
-
-    def finish(i, _):
-        rows = pl.ds(pl.multiple_of(i * BLOCK, BLOCK), BLOCK)
-        for j in range(COLS // BLOCK):
-            cols = pl.ds(j * BLOCK, BLOCK)
-            kept = jnp.full((BLOCK, BLOCK), keep[j, i].astype(jnp.float32))
-            out[rows, cols] = (total[rows, cols] * kept).astype(jnp.bfloat16)
-        return 0
-
-    lax.fori_loop(0, ROWS // BLOCK, finish, 0)
-    for copy in sent:
+    shared_span(P_FAR, 0, 1, 3)
+    total[pl.ds(0, 368)] += product_of(a_late, (0, 368))
+    for k in (1, 4, 6):
+        arrived(b_links, P_FAR, k)
+    finish((0, 384), product_of(b_late, (0, 384)))
+    finish(
+        (384, 640),
+        part_of(b_late, (384, 640), (0, 128)) + part_of(b_late, (384, 640), (640, 128)),
+    )
+    for copy in sent[len(ringed):]:
         copy.wait_send()
 
 

time: 78.9 us -> 77.7 us (0.985)
  Pallas kernels: 77.8 us -> 76.6 us
    pallas_call x1, Pallas kernels: 77.8 us -> 76.6 us  [on_device(): pl.pallas_call(kernel, out_shape=jax.ShapeDtypeStruct((ROWS, COLS), jnp.b...]
where the time goes in v4:
time: 77.7 us; the launch traced here: 77.5 us
  Pallas kernels  76.6 us (99%)
  local copies, waits for them, and re-layouts  0.97 us (1%)
    pallas_call x1, Pallas kernels, on_device(): pl.pallas_call(kernel, out_shape=jax.ShapeDtypeStruct((ROWS, COLS), jnp.b...  76.6 us

profile of v4, /device:TPU:1, one launch (start us, length us, event | category | flops | bytes accessed | tf_op | source)
XLA Modules:
  0.0 77.5 jit_solution(18424537649745820846)
XLA Ops:
  0.0 76.6 %shard_map.55 = bf16[1024,512]{1,0:T(8,128)(2,1)S(1)} custom-call(bf16[1024,512]{1,0:T(8,128)(2,1)} %left_in.1, bf16[1024,512]{1,0:T(8,128)(2,1)} %right_in.1, s32[4,8]{1,0:T(4,128)} %bitcast.3, s32[4,8]{1,0:T(4,128)} %bitcast.4, s32[4,8]{1,0:T(4,128)} %bitcast.5), custom_call_target="tpu_custom_call" | custom-call | tf_op jit(solution)/shard_map/pallas_call | solution.py:358
  76.6 1.0 %copy.7 = bf16[1024,512]{1,0:T(8,128)(2,1)} copy(bf16[1024,512]{1,0:T(8,128)(2,1)S(1)} %shard_map.55) | data formatting | bytes 2097152

commit v5 on v4

--- a/solution.py
+++ b/solution.py
@@ -17,9 +17,9 @@
 RING_STEP = (0, 3, 1, 2, 0, 3, 1, 2)
 
 A_FAR = (
-    ((0, 112), (112, 128)),
-    ((368, 112), (240, 128)),
-    ((480, 272), (752, 272)),
+    ((0, 96), (96, 128)),
+    ((352, 96), (224, 128)),
+    ((448, 288), (736, 288)),
 )
 B_FAR = (
     ((128, 224), (0, 128)),
@@ -139,7 +139,7 @@
 
     a_links = (a_stream, z_up, z_down, a_plane)
     b_links = (b_stream, x_up, x_down, b_plane)
-    both = (b_links, a_links)
+    both = (a_links, b_links)
 
     def share(origin, index):
         c_stream.send(origin, a_stream.spans(origin)[index], sibling, origin, index)
@@ -268,14 +268,14 @@
     for copy in patterns[:2]:
         copy.wait()
     for i in range(PIECES):
+        loads[2 * i + 1].wait()
+        mask(a_all.at[a_own, core], a_pat, i)
+        if i == 0:
+            pl.semaphore_wait(barrier, len(partners))
+        send_own(a_links, i)
         loads[2 * i].wait()
         mask(b_all.at[b_own], b_pat, i)
-        if i == 0:
-            pl.semaphore_wait(barrier, len(partners))
         send_own(b_links, i)
-        loads[2 * i + 1].wait()
-        mask(a_all.at[a_own, core], a_pat, i)
-        send_own(a_links, i)
 
     for i in range(PIECES):
         for links in both:
@@ -287,7 +287,7 @@
         for links in both:
             for index in dict.fromkeys((i, j)):
                 arrived(links, FAR, index)
-    for links in both[::-1]:
+    for links in both:
         plane_far(links)
     for links in both:
         plane_step(links, PIECES - 1)
@@ -328,7 +328,7 @@
     for k in (1, 3):
         arrived(a_links, P_FAR, k)
     shared_span(P_FAR, 2, 4, 5)
-    total[pl.ds(368, 656)] += product_of(a_late, (368, 656))
+    total[pl.ds(352, 672)] += product_of(a_late, (352, 672))
     for k in (0, 2):
         arrived(b_links, P_FAR, k)
     add(b_late, (384, 640), (128, 384))
@@ -339,7 +339,7 @@
     )
     patterns[2].wait()
     shared_span(P_FAR, 0, 1, 3)
-    total[pl.ds(0, 368)] += product_of(a_late, (0, 368))
+    total[pl.ds(0, 352)] += product_of(a_late, (0, 352))
     for k in (1, 4, 6):
         arrived(b_links, P_FAR, k)
     finish((0, 384), product_of(b_late, (0, 384)))

time: 77.7 us -> 77.3 us (level)
  no operation moved by 1% of the time
where the time goes in v5:
time: 77.3 us; the launch traced here: 77.2 us
  Pallas kernels  76.2 us (99%)
  local copies, waits for them, and re-layouts  0.97 us (1%)
    pallas_call x1, Pallas kernels, on_device(): pl.pallas_call(kernel, out_shape=jax.ShapeDtypeStruct((ROWS, COLS), jnp.b...  76.2 us

profile of v5, /device:TPU:1, one launch (start us, length us, event | category | flops | bytes accessed | tf_op | source)
XLA Modules:
  0.0 77.2 jit_solution(5920107713864869595)
XLA Ops:
  0.0 76.2 %shard_map.55 = bf16[1024,512]{1,0:T(8,128)(2,1)S(1)} custom-call(bf16[1024,512]{1,0:T(8,128)(2,1)} %left_in.1, bf16[1024,512]{1,0:T(8,128)(2,1)} %right_in.1, s32[4,8]{1,0:T(4,128)} %bitcast.3, s32[4,8]{1,0:T(4,128)} %bitcast.4, s32[4,8]{1,0:T(4,128)} %bitcast.5), custom_call_target="tpu_custom_call" | custom-call | tf_op jit(solution)/shard_map/pallas_call | solution.py:358
  76.2 1.0 %copy.7 = bf16[1024,512]{1,0:T(8,128)(2,1)} copy(bf16[1024,512]{1,0:T(8,128)(2,1)S(1)} %shard_map.55) | data formatting | bytes 2097152

commit v6 on v5

--- a/solution.py
+++ b/solution.py
@@ -328,7 +328,7 @@
     for k in (1, 3):
         arrived(a_links, P_FAR, k)
     shared_span(P_FAR, 2, 4, 5)
-    total[pl.ds(352, 672)] += product_of(a_late, (352, 672))
+    total[pl.ds(384, 640)] += product_of(a_late, (384, 640))
     for k in (0, 2):
         arrived(b_links, P_FAR, k)
     add(b_late, (384, 640), (128, 384))
@@ -339,10 +339,9 @@
     )
     patterns[2].wait()
     shared_span(P_FAR, 0, 1, 3)
-    total[pl.ds(0, 352)] += product_of(a_late, (0, 352))
     for k in (1, 4, 6):
         arrived(b_links, P_FAR, k)
-    finish((0, 384), product_of(b_late, (0, 384)))
+    finish((0, 384), product_of(a_late, (0, 384)) + product_of(b_late, (0, 384)))
     finish(
         (384, 640),
         part_of(b_late, (384, 640), (0, 128)) + part_of(b_late, (384, 640), (640, 128)),

time: 77.3 us -> 77.3 us (level)
  no operation moved by 1% of the time
where the time goes in v6:
time: 77.3 us; the launch traced here: 77.1 us
  Pallas kernels  76.2 us (99%)
  local copies, waits for them, and re-layouts  0.97 us (1%)
    pallas_call x1, Pallas kernels, on_device(): pl.pallas_call(kernel, out_shape=jax.ShapeDtypeStruct((ROWS, COLS), jnp.b...  76.2 us

profile of v6, /device:TPU:1, one launch (start us, length us, event | category | flops | bytes accessed | tf_op | source)
XLA Modules:
  0.0 77.1 jit_solution(12430052967905965563)
XLA Ops:
  0.0 76.2 %shard_map.55 = bf16[1024,512]{1,0:T(8,128)(2,1)S(1)} custom-call(bf16[1024,512]{1,0:T(8,128)(2,1)} %left_in.1, bf16[1024,512]{1,0:T(8,128)(2,1)} %right_in.1, s32[4,8]{1,0:T(4,128)} %bitcast.3, s32[4,8]{1,0:T(4,128)} %bitcast.4, s32[4,8]{1,0:T(4,128)} %bitcast.5), custom_call_target="tpu_custom_call" | custom-call | tf_op jit(solution)/shard_map/pallas_call | solution.py:357
  76.2 1.0 %copy.7 = bf16[1024,512]{1,0:T(8,128)(2,1)} copy(bf16[1024,512]{1,0:T(8,128)(2,1)S(1)} %shard_map.55) | data formatting | bytes 2097152

commit v7 on v6

--- a/solution.py
+++ b/solution.py
@@ -22,9 +22,9 @@
     ((448, 288), (736, 288)),
 )
 B_FAR = (
-    ((128, 224), (0, 128)),
-    ((352, 160), (512, 128), (640, 64)),
-    ((768, 256), (704, 64)),
+    ((128, 208), (0, 128)),
+    ((336, 176), (512, 128), (640, 32)),
+    ((768, 256), (672, 96)),
 )
 PER_ORIGIN = 8
 ALL = (0, ROWS)

time: 77.3 us -> 77.8 us (level)
  no operation moved by 1% of the time
where the time goes in v7:
time: 77.8 us; the launch traced here: 77.7 us
  Pallas kernels  76.7 us (99%)
  local copies, waits for them, and re-layouts  0.97 us (1%)
    pallas_call x1, Pallas kernels, on_device(): pl.pallas_call(kernel, out_shape=jax.ShapeDtypeStruct((ROWS, COLS), jnp.b...  76.7 us

profile of v7, /device:TPU:1, one launch (start us, length us, event | category | flops | bytes accessed | tf_op | source)
XLA Modules:
  0.0 77.7 jit_solution(2170269927688352127)
XLA Ops:
  0.0 76.7 %shard_map.55 = bf16[1024,512]{1,0:T(8,128)(2,1)S(1)} custom-call(bf16[1024,512]{1,0:T(8,128)(2,1)} %left_in.1, bf16[1024,512]{1,0:T(8,128)(2,1)} %right_in.1, s32[4,8]{1,0:T(4,128)} %bitcast.3, s32[4,8]{1,0:T(4,128)} %bitcast.4, s32[4,8]{1,0:T(4,128)} %bitcast.5), custom_call_target="tpu_custom_call" | custom-call | tf_op jit(solution)/shard_map/pallas_call | solution.py:357
  76.7 1.0 %copy.7 = bf16[1024,512]{1,0:T(8,128)(2,1)} copy(bf16[1024,512]{1,0:T(8,128)(2,1)S(1)} %shard_map.55) | data formatting | bytes 2097152
